TPU v7x, 256 devices: a whole 4x4x8 slice. The times are simulated.
256 devices in a mesh: lon: 64 (over z, x, y_hi), probe: 4 (over y_lo, core).
Axes of the slice: x: 4, y: 4 (y_hi: 2, y_lo: 2; y = y_hi * 2 + y_lo), z: 8, core: 2. Of those that a mesh axis runs over, the one named last changes fastest.
Arguments:
- increments: float32 [64, 1536, 8, 256], P('probe', 'lon'), may hold values from -6 to 6
- winds: float32 [2, 1536, 8, 256], P(None, 'lon'), may hold values from -0.2 to 0.2
- obs_weight: float32 [1536, 8, 256], P('lon'), may hold values from 0.1 to 10
Outputs:
- basis: float32 [64, 384, 512], P('probe', 'lon')
- upper: float32 [64, 64], replicated
All inputs are finite; a program needn't handle non-finite values.
Results may differ from a plain program's by a relative error of at most 0.00011.
Values sent between devices are 32-bit elements; how exact they have to be, the bound alone decides.
A program may use at most 128 MiB of HBM per device.

v0:
```python
import jax
import jax.numpy as jnp
from jax import lax
from jax.sharding import PartitionSpec as P


def from_behind(block, axis, distance):
    devices = range(lax.axis_size(axis))
    route = [((i - distance) % len(devices), i) for i in devices]
    return lax.ppermute(block, axis, route)


def padded(block, sides, width):
    for axis, dim in sides:
        count = lax.axis_size(axis)
        forward = [(i, i + 1) for i in range(count - 1)]
        forward.append((count - 1, 0))
        backward = [(target, source) for source, target in forward]
        low = lax.ppermute(
            lax.slice_in_dim(block, block.shape[dim] - width, None, axis=dim), axis, forward
        )
        high = lax.ppermute(lax.slice_in_dim(block, 0, width, axis=dim), axis, backward)
        block = jnp.concatenate([low, block, high], axis=dim)
    return block


def lat_mask(field):
    rows = lax.broadcasted_iota(jnp.int32, field.shape, field.ndim - 1)
    return jnp.where(rows > 0, field, jnp.zeros_like(field))


def below(field):
    return jnp.concatenate([jnp.zeros_like(field[..., :1]), field[..., :-1]], axis=-1)


def above(field):
    return jnp.concatenate([field[..., 1:], jnp.zeros_like(field[..., :1])], axis=-1)


def forward_core(widened, east, north):
    a_pos = jnp.maximum(east, 0.0)
    b_neg = jnp.minimum(east, 0.0)
    c_pos = jnp.maximum(north[1:-1], 0.0)
    d_neg = jnp.minimum(north[1:-1], 0.0)
    flux_w = a_pos[1:] * widened[:, :-1] + b_neg[1:] * widened[:, 1:]
    inner = widened[:, 1:-1]
    flux_s = c_pos * below(inner) + d_neg * inner
    flux_n = above(flux_s)
    return inner - (flux_w[:, 1:] - flux_w[:, :-1]) - (flux_n - flux_s)


def adjoint_core(widened, east, north):
    a_pos = jnp.maximum(east, 0.0)
    b_neg = jnp.minimum(east, 0.0)[1:-1]
    c_pos = jnp.maximum(north[1:-1], 0.0)
    d_neg = jnp.minimum(north[1:-1], 0.0)
    a_east = a_pos[2:]
    c_north = above(c_pos)
    inner = widened[:, 1:-1]
    west_val = widened[:, :-2]
    east_val = widened[:, 2:]
    return (
        inner * (1.0 - a_east + b_neg - c_north + d_neg)
        - b_neg * west_val
        + a_east * east_val
        - d_neg * below(inner)
        + c_north * above(inner)
    )


def body(increments, winds, obs_weight):
    east_local = winds[0]
    north_local = lat_mask(winds[1])
    next_first = from_behind(east_local[:1], "lon", -1)
    near_east = jnp.concatenate([jnp.zeros_like(next_first), east_local, next_first], axis=0)
    edge_zero = jnp.zeros_like(north_local[:1])
    near_north = jnp.concatenate([edge_zero, north_local, edge_zero], axis=0)

    def widen(field):
        return padded(field, (("lon", 1),), 1)

    state = increments
    for step in range(2):
        state = forward_core(widen(state), near_east, near_north)
    state = obs_weight * state
    for step in range(2):
        state = adjoint_core(widen(state), near_east, near_north)
    sketch = increments + state
    probe_count, lon_count, level_count, lat_count = sketch.shape
    coarse = jnp.mean(
        sketch.reshape(probe_count, lon_count // 4, 4, level_count, lat_count // 4, 4), axis=(2, 5)
    )
    coarse = coarse.reshape(probe_count, -1)
    all_probes = probe_count * lax.axis_size("probe")
    ident = jnp.eye(all_probes, dtype=jnp.float32)
    full_panel = lax.all_gather(coarse, "probe", axis=0, tiled=True)
    local_gram = jnp.dot(
        full_panel,
        full_panel.T,
        precision=lax.Precision.HIGHEST,
        preferred_element_type=jnp.float32,
    )
    gram = lax.psum(local_gram, "lon")
    lower = jnp.linalg.cholesky(gram)
    inverse = lax.linalg.triangular_solve(lower, ident, left_side=True, lower=True)
    own_rows = lax.dynamic_slice_in_dim(
        inverse, lax.axis_index("probe") * probe_count, probe_count, 0
    )
    basis = jnp.dot(
        own_rows, full_panel, precision=lax.Precision.HIGHEST, preferred_element_type=jnp.float32
    )
    return (basis.reshape(probe_count, lon_count // 4, -1), lower.T)


def solution(mesh):
    in_specs = (P("probe", "lon", None, None), P(None, "lon", None, None), P("lon", None, None))
    out_specs = (P("probe", "lon", None), P())
    return jax.shard_map(body, mesh=mesh, in_specs=in_specs, out_specs=out_specs, check_vma=False)
```

profile of v0, /device:TPU:8, one launch (start us, length us, event | category | flops | bytes accessed | tf_op | source)
XLA Modules:
  0.0 485.5 jit_solution(4162303472473665741)
XLA Ops:
  0.6 0.7 slice_bitcast_fusion.1
  1.3 9.8 %collective-permute-start = (f32[1,8,256]{2,1,0:T(8,128)S(1)}, f32[1,8,256]{2,1,0:T(8,128)S(1)}, u32[]{:S(2)}, u32[]{:S(2)}) collective-permute-start(f32[1,8,256]{2,1,0:T(8,128)S(1)} %slice_bitcast_fusion.1), channel_id=1, source_target_pairs={{4,0},{8,4},{12,8},{16,12},{20,16},{24,20},{28,24},{32,28},{36,32}... | collective-permute-start | bytes 24584 | tf_op jit(solution)/shard_map/ppermute | solution.py:10
  11.1 1.7 fusion.34
  12.8 0.0 collective-permute-start.1
  12.8 7.7 %collective-permute-start.2 = (f32[16,1,8,256]{3,2,1,0:T(8,128)}, f32[16,1,8,256]{3,2,1,0:T(8,128)}, u32[]{:S(2)}, u32[]{:S(2)}) collective-permute-start(f32[16,1,8,256]{3,2,1,0:T(8,128)} %get-tuple-element.22), channel_id=1, source_target_pairs={{4,0},{8,4},{12,8},{16,12},{20,16},{24,20},{28,24},{32,28},{36,32}... | collective-permute-start | bytes 393224 | tf_op jit(solution)/shard_map/ppermute | solution.py:22
  20.6 1.1 maximum_bitcast_fusion
  21.6 0.0 copy-start.4
  21.6 1.0 bitcast_select_fusion
  22.7 3.8 multiply_add_fusion.1
  26.5 0.0 copy-done.7
  26.5 0.0 copy-done.4
  26.5 0.0 copy-start.1
  26.5 0.9 slice_maximum_fusion
  27.4 0.8 copy-done.1
  28.2 2.6 slice.164
  30.7 0.5 pad.25.clone
  31.2 0.0 collective-permute-done
  31.3 0.7 fusion.21
  32.1 1.1 minimum_add_fusion
  33.2 0.0 collective-permute-done.1
  33.2 0.0 collective-permute-done.2
  33.2 0.0 copy-done
  33.2 1.5 fusion
  34.7 0.5 copy-done.2
  35.2 1.0 copy-done.3
  36.1 0.9 fusion.19
  37.1 0.1 collective-permute-start.3
  37.1 7.7 %collective-permute-start.4 = (f32[16,1,8,256]{3,2,1,0:T(8,128)S(1)}, f32[16,1,8,256]{3,2,1,0:T(8,128)S(1)}, u32[]{:S(2)}, u32[]{:S(2)}) collective-permute-start(f32[16,1,8,256]{3,2,1,0:T(8,128)S(1)} %get-tuple-element.20), channel_id=1, source_target_pairs={{4,0},{8,4},{12,8},{16,12},{20,16},{24,20},{28,24},{32,28},{36,32}... | collective-permute-start | bytes 393224 | tf_op jit(solution)/shard_map/ppermute | solution.py:22
  44.9 0.0 copy-done.5
  44.9 1.0 multiply_add_fusion
  45.9 2.5 slice.170
  48.4 0.0 collective-permute-done.3
  48.4 0.0 collective-permute-done.4
  48.4 0.4 fusion.1
  48.8 0.5 copy-done.6
  49.3 2.8 fusion.17
  52.2 0.1 collective-permute-start.5
  52.3 7.7 %collective-permute-start.6 = (f32[16,1,8,256]{3,2,1,0:T(8,128)S(1)}, f32[16,1,8,256]{3,2,1,0:T(8,128)S(1)}, u32[]{:S(2)}, u32[]{:S(2)}) collective-permute-start(f32[16,1,8,256]{3,2,1,0:T(8,128)S(1)} %get-tuple-element.19), channel_id=1, source_target_pairs={{4,0},{8,4},{12,8},{16,12},{20,16},{24,20},{28,24},{32,28},{36,32}... | collective-permute-start | bytes 393224 | tf_op jit(solution)/shard_map/ppermute | solution.py:22
  60.0 1.1 fusion.31
  61.1 1.8 collective-permute-done.5
  63.0 0.0 collective-permute-done.6
  63.0 2.2 fusion.12
  65.2 0.1 collective-permute-start.7
  65.3 7.8 %collective-permute-start.8 = (f32[16,1,8,256]{3,2,1,0:T(8,128)S(1)}, f32[16,1,8,256]{3,2,1,0:T(8,128)S(1)}, u32[]{:S(2)}, u32[]{:S(2)}) collective-permute-start(f32[16,1,8,256]{3,2,1,0:T(8,128)S(1)} %get-tuple-element.15), channel_id=1, source_target_pairs={{4,0},{8,4},{12,8},{16,12},{20,16},{24,20},{28,24},{32,28},{36,32}... | collective-permute-start | bytes 393224 | tf_op jit(solution)/shard_map/ppermute | solution.py:22
  73.1 1.2 fusion.29
  74.3 1.7 collective-permute-done.7
  76.0 0.0 collective-permute-done.8
  76.0 3.7 fusion.6
  79.6 13.4 %copy.25 = f32[16,24,8,256]{0,2,3,1:T(8,128)} copy(f32[16,24,8,256]{3,2,1,0:T(8,128)} %fusion.6) | data formatting | bytes 6291456 | tf_op jit(solution)/shard_map/add | solution.py:88
  93.0 10.1 %reduce_sum.9 = f32[16,6,8,64]{0,2,3,1:T(8,128)S(1)} reduce(f32[16,6,4,8,64,4]{0,3,5,4,2,1:T(8,128)} %bitcast.36, f32[]{:T(128)} %constant.53.clone.1), dimensions={2,5}, to_apply=%region_0.1 | reduce | flops 737280 | bytes 3342340 | tf_op jit(solution)/shard_map/reduce_sum | solution.py:90
  103.2 0.5 copy.26
  103.7 0.2 div.18
  103.9 8.5 %all_gather.3 = f32[64,3072]{1,0:T(8,128)S(1)} all-gather(f32[16,3072]{1,0:T(8,128)S(1)} %div.18), channel_id=1, replica_groups=mesh['lon'=64,'probe'=4] {'probe'}, dimensions={0}, use_global_device_ids=true | all-gather | bytes 983040 | tf_op jit(solution)/shard_map/all_gather | solution.py:96
  112.3 0.8 fusion.35
  113.1 358.1 %psum.7 = f32[64,64]{0,1:T(8,128)S(1)} all-reduce(f32[64,64]{0,1:T(8,128)S(1)} %fusion.35), channel_id=1, replica_groups=mesh['lon'=64,'probe'=4] {'lon'}, use_global_device_ids=true, to_apply=%region_1.2 | all-reduce | flops 4096 | bytes 32768 | tf_op jit(solution)/shard_map/psum | solution.py:103
  471.2 0.1 copy.28
  471.2 5.8 %cholesky.17 = f32[64,64]{1,0:T(8,128)S(1)} custom-call(f32[64,64]{1,0:T(8,128)S(1)} %fusion.24), custom_call_target="Cholesky" | custom-call | tf_op jit(solution)/shard_map/jit(cholesky)/cholesky | solution.py:104
  477.1 0.6 compare_reduce_fusion
  477.8 0.7 fusion.25
  478.4 4.9 %custom-call.6 = f32[1,64,64]{1,2,0:T(8,128)S(1)} custom-call(f32[1,64,64]{2,1,0:T(8,128)S(1)} %get-tuple-element.34), custom_call_target="InvertDiagBlocksLowerTriangular" | custom-call | tf_op jit(solution)/shard_map/triangular_solve | solution.py:105
  483.3 0.2 fusion.22
  483.6 0.5 fusion.26
  484.1 0.7 copy.34
  484.8 0.7 copy.30
  (15 shorter events, 0.2 us)
Async XLA Ops:
  1.3 29.9 %collective-permute-start = (f32[1,8,256]{2,1,0:T(8,128)S(1)}, f32[1,8,256]{2,1,0:T(8,128)S(1)}, u32[]{:S(2)}, u32[]{:S(2)}) collective-permute-start(f32[1,8,256]{2,1,0:T(8,128)S(1)} %slice_bitcast_fusion.1), channel_id=1, source_target_pairs={{4,0},{8,4},{12,8},{16,12},{20,16},{24,20},{28,24},{32,28},{36,32}... | collective-permute-start | bytes 24584 | tf_op jit(solution)/shard_map/ppermute | solution.py:10
  12.8 20.4 %collective-permute-start.1 = (f32[16,1,8,256]{3,2,1,0:T(8,128)}, f32[16,1,8,256]{3,2,1,0:T(8,128)}, u32[]{:S(2)}, u32[]{:S(2)}) collective-permute-start(f32[16,1,8,256]{3,2,1,0:T(8,128)} %get-tuple-element.23), channel_id=1, source_target_pairs={{0,4},{4,8},{8,12},{12,16},{16,20},{20,24},{24,28},{28,32},{32,36}... | collective-permute-start | bytes 393224 | tf_op jit(solution)/shard_map/ppermute | solution.py:19
  12.8 20.4 %collective-permute-start.2 = (f32[16,1,8,256]{3,2,1,0:T(8,128)}, f32[16,1,8,256]{3,2,1,0:T(8,128)}, u32[]{:S(2)}, u32[]{:S(2)}) collective-permute-start(f32[16,1,8,256]{3,2,1,0:T(8,128)} %get-tuple-element.22), channel_id=1, source_target_pairs={{4,0},{8,4},{12,8},{16,12},{20,16},{24,20},{28,24},{32,28},{36,32}... | collective-permute-start | bytes 393224 | tf_op jit(solution)/shard_map/ppermute | solution.py:22
  20.6 5.9 %copy-start.7 = (pred[256]{0:T(512)(128)(4,1)}, pred[256]{0:T(512)(128)(4,1)S(1)}, u32[]{:S(2)}) copy-start(pred[256]{0:T(512)(128)(4,1)S(1)} %iota_compare_fusion.3) | copy-start | bytes 772
  21.6 4.8 copy-start.4
  26.5 1.7 copy-start.1
  28.2 5.0 %copy-start = (f32[16,24,8,256]{3,2,1,0:T(8,128)S(1)}, f32[16,24,8,256]{3,2,1,0:T(8,128)}, u32[]{:S(2)}) copy-start(f32[16,24,8,256]{3,2,1,0:T(8,128)} %param.3) | copy-start | bytes 9437188
  33.2 2.0 copy-start.2
  33.2 3.0 copy-start.3
  36.1 8.8 %copy-start.5 = (f32[24,8,256]{2,1,0:T(8,128)S(1)}, f32[24,8,256]{2,1,0:T(8,128)}, u32[]{:S(2)}) copy-start(f32[24,8,256]{2,1,0:T(8,128)} %copy-done.4) | copy-start | bytes 589828
  37.1 11.3 %collective-permute-start.3 = (f32[16,1,8,256]{3,2,1,0:T(8,128)S(1)}, f32[16,1,8,256]{3,2,1,0:T(8,128)S(1)}, u32[]{:S(2)}, u32[]{:S(2)}) collective-permute-start(f32[16,1,8,256]{3,2,1,0:T(8,128)S(1)} %get-tuple-element.21), channel_id=1, source_target_pairs={{0,4},{4,8},{8,12},{12,16},{16,20},{20,24},{24,28},{28,32},{32,36}... | collective-permute-start | bytes 393224 | tf_op jit(solution)/shard_map/ppermute | solution.py:19
  37.1 11.2 %collective-permute-start.4 = (f32[16,1,8,256]{3,2,1,0:T(8,128)S(1)}, f32[16,1,8,256]{3,2,1,0:T(8,128)S(1)}, u32[]{:S(2)}, u32[]{:S(2)}) collective-permute-start(f32[16,1,8,256]{3,2,1,0:T(8,128)S(1)} %get-tuple-element.20), channel_id=1, source_target_pairs={{4,0},{8,4},{12,8},{16,12},{20,16},{24,20},{28,24},{32,28},{36,32}... | collective-permute-start | bytes 393224 | tf_op jit(solution)/shard_map/ppermute | solution.py:22
  48.4 0.9 copy-start.6
  52.2 10.8 %collective-permute-start.5 = (f32[16,1,8,256]{3,2,1,0:T(8,128)S(1)}, f32[16,1,8,256]{3,2,1,0:T(8,128)S(1)}, u32[]{:S(2)}, u32[]{:S(2)}) collective-permute-start(f32[16,1,8,256]{3,2,1,0:T(8,128)S(1)} %get-tuple-element.18), channel_id=1, source_target_pairs={{0,4},{4,8},{8,12},{12,16},{16,20},{20,24},{24,28},{28,32},{32,36}... | collective-permute-start | bytes 393224 | tf_op jit(solution)/shard_map/ppermute | solution.py:19
  52.3 10.7 %collective-permute-start.6 = (f32[16,1,8,256]{3,2,1,0:T(8,128)S(1)}, f32[16,1,8,256]{3,2,1,0:T(8,128)S(1)}, u32[]{:S(2)}, u32[]{:S(2)}) collective-permute-start(f32[16,1,8,256]{3,2,1,0:T(8,128)S(1)} %get-tuple-element.19), channel_id=1, source_target_pairs={{4,0},{8,4},{12,8},{16,12},{20,16},{24,20},{28,24},{32,28},{36,32}... | collective-permute-start | bytes 393224 | tf_op jit(solution)/shard_map/ppermute | solution.py:22
  65.2 10.8 %collective-permute-start.7 = (f32[16,1,8,256]{3,2,1,0:T(8,128)S(1)}, f32[16,1,8,256]{3,2,1,0:T(8,128)S(1)}, u32[]{:S(2)}, u32[]{:S(2)}) collective-permute-start(f32[16,1,8,256]{3,2,1,0:T(8,128)S(1)} %get-tuple-element.14), channel_id=1, source_target_pairs={{0,4},{4,8},{8,12},{12,16},{16,20},{20,24},{24,28},{28,32},{32,36}... | collective-permute-start | bytes 393224 | tf_op jit(solution)/shard_map/ppermute | solution.py:19
  65.3 10.7 %collective-permute-start.8 = (f32[16,1,8,256]{3,2,1,0:T(8,128)S(1)}, f32[16,1,8,256]{3,2,1,0:T(8,128)S(1)}, u32[]{:S(2)}, u32[]{:S(2)}) collective-permute-start(f32[16,1,8,256]{3,2,1,0:T(8,128)S(1)} %get-tuple-element.15), channel_id=1, source_target_pairs={{4,0},{8,4},{12,8},{16,12},{20,16},{24,20},{28,24},{32,28},{36,32}... | collective-permute-start | bytes 393224 | tf_op jit(solution)/shard_map/ppermute | solution.py:22
where the time goes:
time: 486 us; the launch traced here: 485 us
  blocking collectives  367 us (76%)
  other arithmetic  43.3 us (9%)
  starting transfers between devices  41.1 us (8%)
  local copies, waits for them, and re-layouts  28.6 us (6%)
    psum x1, blocking collectives, body(): gram = lax.psum(local_gram, 'lon')  358 us
    ppermute x4, starting transfers between devices, padded(): lax.ppermute(lax.slice_in_dim(block, 0, width, axis=dim), axis, backward)  31 us
    add x1, local copies, waits for them, and re-layouts, body(): sketch = increments + state  13.4 us
    reduce_sum x1, other arithmetic, body(): jnp.mean(sketch.reshape(probe_count, lon_count // 4, 4, level_count, lat_...  10.1 us
    ppermute x1, starting transfers between devices, from_behind(): return lax.ppermute(block, axis, route)  9.78 us
  transfers between devices with their start and end apart: 9, of which 2 were waited for; matrix products, arithmetic and copies ran while one was open for 4% of the time, Pallas kernels for 0%

commit v1 on v0

--- a/solution.py
+++ b/solution.py
@@ -100,7 +100,7 @@
         precision=lax.Precision.HIGHEST,
         preferred_element_type=jnp.float32,
     )
-    gram = lax.psum(local_gram, "lon")
+    gram = jnp.sum(lax.all_gather(local_gram, "lon"), axis=0)
     lower = jnp.linalg.cholesky(gram)
     inverse = lax.linalg.triangular_solve(lower, ident, left_side=True, lower=True)
     own_rows = lax.dynamic_slice_in_dim(

time: 486 us -> 251 us (0.52)
  blocking collectives: 367 us -> 8.45 us
  waiting for transfers between devices: 3.54 us -> 120 us
  between operations: 0.92 us -> 14.4 us
  local copies, waits for them, and re-layouts: 28.6 us -> 23.1 us
    psum x1 -> x0, blocking collectives: 358 us -> none  [body(): gram = lax.psum(local_gram, 'lon')]
    all_gather x0 -> x1, waiting for transfers between devices: none -> 116 us  [body(): gram = jnp.sum(lax.all_gather(local_gram, 'lon'), axis=0)]
  transfers between devices with their start and end apart: 9 -> 10, of which waited for: 2 -> 3; matrix products, arithmetic and copies ran while one was open for 4% -> 5% of each run, Pallas kernels for 0% -> 0%
where the time goes in v1:
time: 251 us; the launch traced here: 250 us
  waiting for transfers between devices  120 us (48%)
  starting transfers between devices  41.2 us (16%)
  other arithmetic  40.5 us (16%)
  local copies, waits for them, and re-layouts  23.1 us (9%)
  between operations  14.4 us (6%)
  blocking collectives  8.45 us (3%)
    all_gather x1, waiting for transfers between devices, body(): gram = jnp.sum(lax.all_gather(local_gram, 'lon'), axis=0)  116 us
    ppermute x4, starting transfers between devices, padded(): lax.ppermute(lax.slice_in_dim(block, 0, width, axis=dim), axis, backward)  31 us
    add x1, local copies, waits for them, and re-layouts, body(): sketch = increments + state  12.1 us
    reduce_sum x1, other arithmetic, body(): jnp.mean(sketch.reshape(probe_count, lon_count // 4, 4, level_count, lat_...  10.1 us
    ppermute x1, starting transfers between devices, from_behind(): return lax.ppermute(block, axis, route)  9.78 us
    all_gather x1, blocking collectives, body(): full_panel = lax.all_gather(coarse, 'probe', axis=0, tiled=True)  8.45 us
    another operation x3, other arithmetic, body(): lower = jnp.linalg.cholesky(gram)  6.52 us
  transfers between devices with their start and end apart: 10, of which 3 were waited for; matrix products, arithmetic and copies ran while one was open for 5% of the time, Pallas kernels for 0%

profile of v1, /device:TPU:8, one launch (start us, length us, event | category | flops | bytes accessed | tf_op | source)
XLA Modules:
  0.0 249.5 jit_solution(16360069103900305089)
XLA Ops:
  7.2 0.0 all-gather.3.cloned.1.call-start
  7.2 0.7 slice_bitcast_fusion.1
  7.9 9.8 %collective-permute-start = (f32[1,8,256]{2,1,0:T(8,128)S(1)}, f32[1,8,256]{2,1,0:T(8,128)S(1)}, u32[]{:S(2)}, u32[]{:S(2)}) collective-permute-start(f32[1,8,256]{2,1,0:T(8,128)S(1)} %slice_bitcast_fusion.1), channel_id=1, source_target_pairs={{4,0},{8,4},{12,8},{16,12},{20,16},{24,20},{28,24},{32,28},{36,32}... | collective-permute-start | bytes 24584 | tf_op jit(solution)/shard_map/ppermute | solution.py:10
  17.7 1.0 fusion.34
  18.7 0.1 collective-permute-start.1
  18.8 7.7 %collective-permute-start.2 = (f32[16,1,8,256]{3,2,1,0:T(8,128)S(1)}, f32[16,1,8,256]{3,2,1,0:T(8,128)S(1)}, u32[]{:S(2)}, u32[]{:S(2)}) collective-permute-start(f32[16,1,8,256]{3,2,1,0:T(8,128)S(1)} %get-tuple-element.22), channel_id=1, source_target_pairs={{4,0},{8,4},{12,8},{16,12},{20,16},{24,20},{28,24},{32,28},{36,32}... | collective-permute-start | bytes 393224 | tf_op jit(solution)/shard_map/ppermute | solution.py:22
  26.5 1.1 maximum_bitcast_fusion
  27.6 0.9 bitcast_select_fusion
  28.5 3.7 %multiply_add_fusion.1 = f32[16,24,8,256]{3,2,1,0:T(8,128)S(1)} fusion(f32[16,24,8,256]{3,2,1,0:T(8,128)} %param.3, f32[16,24,8,255]{3,2,1,0:T(8,128)} %bitcast.38, f32[24,8,256]{2,1,0:T(8,128)S(1)} %get-tuple-element.25, f32[24,8,256]{2,1,0:T(8,128)S(1)} %get-tuple-element.24), kind=kLoop, calls=%fused_computation.31 | loop fusion | flops 2359296 | bytes 9818112 | tf_op jit(solution)/shard_map/add | solution.py:47
  32.3 0.1 slice_maximum_fusion
  32.4 0.0 copy-start.7
  32.4 0.0 copy-start
  32.4 0.9 slice.164
  33.3 0.0 collective-permute-done
  33.3 0.1 fusion.21
  33.5 0.1 minimum_add_fusion
  33.6 0.0 copy-start.5
  33.6 0.0 collective-permute-done.1
  33.6 0.0 collective-permute-done.2
  33.6 0.8 copy-done
  34.4 0.4 fusion
  34.8 1.0 fusion.19
  35.8 0.1 collective-permute-start.3
  35.9 7.7 %collective-permute-start.4 = (f32[16,1,8,256]{3,2,1,0:T(8,128)S(1)}, f32[16,1,8,256]{3,2,1,0:T(8,128)S(1)}, u32[]{:S(2)}, u32[]{:S(2)}) collective-permute-start(f32[16,1,8,256]{3,2,1,0:T(8,128)S(1)} %get-tuple-element.20), channel_id=1, source_target_pairs={{4,0},{8,4},{12,8},{16,12},{20,16},{24,20},{28,24},{32,28},{36,32}... | collective-permute-start | bytes 393224 | tf_op jit(solution)/shard_map/ppermute | solution.py:22
  43.7 1.0 multiply_add_fusion
  44.6 2.5 %slice.170 = f32[16,24,8,255]{3,2,1,0:T(8,128)} slice(f32[16,24,8,256]{3,2,1,0:T(8,128)S(1)} %multiply_add_fusion), slice={[0:16], [0:24], [0:8], [1:256]} | slice | bytes 6266880 | tf_op jit(solution)/shard_map/slice | solution.py:37
  47.2 0.0 collective-permute-done.3
  47.2 0.0 collective-permute-done.4
  47.2 0.4 fusion.1
  47.6 0.5 copy-done.8
  48.1 2.8 %fusion.17 = f32[16,24,8,256]{3,2,1,0:T(8,128)S(1)} fusion(f32[16,24,8,256]{3,2,1,0:T(8,128)S(1)} %fusion.19, f32[16,25,8,256]{3,2,1,0:T(8,128)S(1)} %fusion.1, f32[16,24,8,256]{3,2,1,0:T(8,128)S(1)} %multiply_add_fusion, f32[16,24,8,255]{3,2,1,0:T(8,128)} %slice.170, f32[24,8,256]{2,1,0:T(8,128)S(1)} %copy-done.8), kind=kLoop, calls=%fused_computation.26 | loop fusion | flops 3932160 | bytes 19058688 | tf_op jit(solution)/shard_map/mul | solution.py:85
  51.0 0.1 collective-permute-start.5
  51.0 7.7 %collective-permute-start.6 = (f32[16,1,8,256]{3,2,1,0:T(8,128)S(1)}, f32[16,1,8,256]{3,2,1,0:T(8,128)S(1)}, u32[]{:S(2)}, u32[]{:S(2)}) collective-permute-start(f32[16,1,8,256]{3,2,1,0:T(8,128)S(1)} %get-tuple-element.19), channel_id=1, source_target_pairs={{4,0},{8,4},{12,8},{16,12},{20,16},{24,20},{28,24},{32,28},{36,32}... | collective-permute-start | bytes 393224 | tf_op jit(solution)/shard_map/ppermute | solution.py:22
  58.8 1.1 fusion.31
  59.9 1.8 collective-permute-done.5
  61.7 0.0 collective-permute-done.6
  61.7 0.0 copy-done.5
  61.7 2.2 fusion.12
  64.0 0.1 collective-permute-start.7
  64.1 0.0 copy-start.2
  64.1 0.0 copy-start.6
  64.1 7.8 %collective-permute-start.8 = (f32[16,1,8,256]{3,2,1,0:T(8,128)S(1)}, f32[16,1,8,256]{3,2,1,0:T(8,128)S(1)}, u32[]{:S(2)}, u32[]{:S(2)}) collective-permute-start(f32[16,1,8,256]{3,2,1,0:T(8,128)S(1)} %get-tuple-element.15), channel_id=1, source_target_pairs={{4,0},{8,4},{12,8},{16,12},{20,16},{24,20},{28,24},{32,28},{36,32}... | collective-permute-start | bytes 393224 | tf_op jit(solution)/shard_map/ppermute | solution.py:22
  71.9 1.2 fusion.29
  73.1 1.7 collective-permute-done.7
  74.8 0.0 collective-permute-done.8
  74.8 2.6 %fusion.6 = f32[16,24,8,256]{3,2,1,0:T(8,128)S(1)} fusion(f32[16,24,8,256]{3,2,1,0:T(8,128)S(1)} %copy-done, f32[16,1,8,256]{3,2,1,0:T(8,128)S(1)} %collective-permute-done.8, f32[16,24,8,256]{3,2,1,0:T(8,128)S(1)} %fusion.12, f32[16,1,8,256]{3,2,1,0:T(8,128)S(1)} %collective-permute-done.7, f32[16,24,8,255]{3,2,1,0:T(8,128)S(1)} %get-tuple-element.13, ...), kind=kLoop, calls=%fused_computation.11 | loop fusion | flops 9437184 | bytes 16949248 | tf_op jit(solution)/shard_map/add | solution.py:88
  77.4 12.1 %copy.21 = f32[16,24,8,256]{0,2,3,1:T(8,128)} copy(f32[16,24,8,256]{3,2,1,0:T(8,128)S(1)} %fusion.6) | data formatting | bytes 6291456 | tf_op jit(solution)/shard_map/add | solution.py:88
  89.5 10.1 %reduce_sum.18 = f32[16,6,8,64]{0,2,3,1:T(8,128)S(1)} reduce(f32[16,6,4,8,64,4]{0,3,5,4,2,1:T(8,128)} %bitcast.37, f32[]{:T(128)} %constant.53.clone.1), dimensions={2,5}, to_apply=%region_0.1 | reduce | flops 737280 | bytes 3342340 | tf_op jit(solution)/shard_map/reduce_sum | solution.py:90
  99.7 0.5 copy.22
  100.2 0.2 div.18
  100.4 8.5 %all_gather.9 = f32[64,3072]{1,0:T(8,128)S(1)} all-gather(f32[16,3072]{1,0:T(8,128)S(1)} %div.18), channel_id=1, replica_groups=mesh['lon'=64,'probe'=4] {'probe'}, dimensions={0}, use_global_device_ids=true | all-gather | bytes 983040 | tf_op jit(solution)/shard_map/all_gather | solution.py:96
  108.8 1.4 fusion.35
  110.2 0.0 all-gather.3.cloned.1.call-update
  110.3 116.3 %all-gather.3.cloned.1.call-done = f32[4096,64]{1,0:T(8,128)} async-done(((f32[64,64]{1,0:T(8,128)}), f32[4096,64]{1,0:T(8,128)}) %all-gather.3.cloned.1.call-update) | async-done | bytes 1048592 | tf_op jit(solution)/shard_map/all_gather | solution.py:103
  226.6 1.8 reduce_sum.19
  228.4 0.1 copy.23
  228.4 5.8 %cholesky.17 = f32[64,64]{1,0:T(8,128)S(1)} custom-call(f32[64,64]{1,0:T(8,128)S(1)} %fusion.24), custom_call_target="Cholesky" | custom-call | tf_op jit(solution)/shard_map/jit(cholesky)/cholesky | solution.py:104
  234.3 0.6 compare_reduce_fusion
  235.0 0.7 fusion.25
  235.6 4.9 %custom-call.6 = f32[1,64,64]{1,2,0:T(8,128)S(1)} custom-call(f32[1,64,64]{2,1,0:T(8,128)S(1)} %get-tuple-element.34), custom_call_target="InvertDiagBlocksLowerTriangular" | custom-call | tf_op jit(solution)/shard_map/triangular_solve | solution.py:105
  240.5 0.2 fusion.22
  240.8 0.5 fusion.26
  241.3 0.7 copy.28
  242.0 0.7 copy.25
  (20 shorter events, 0.2 us)
Async XLA Ops:
  7.2 219.4 %all-gather.3.cloned.1.call-start = ((), (), s32[]{:S(2)}) async-start(), calls=%async_computation | async-start | bytes 2129920 | tf_op jit(solution)/shard_map/all_gather | solution.py:103
  7.9 25.4 %collective-permute-start = (f32[1,8,256]{2,1,0:T(8,128)S(1)}, f32[1,8,256]{2,1,0:T(8,128)S(1)}, u32[]{:S(2)}, u32[]{:S(2)}) collective-permute-start(f32[1,8,256]{2,1,0:T(8,128)S(1)} %slice_bitcast_fusion.1), channel_id=1, source_target_pairs={{4,0},{8,4},{12,8},{16,12},{20,16},{24,20},{28,24},{32,28},{36,32}... | collective-permute-start | bytes 24584 | tf_op jit(solution)/shard_map/ppermute | solution.py:10
  18.7 14.9 %collective-permute-start.1 = (f32[16,1,8,256]{3,2,1,0:T(8,128)S(1)}, f32[16,1,8,256]{3,2,1,0:T(8,128)S(1)}, u32[]{:S(2)}, u32[]{:S(2)}) collective-permute-start(f32[16,1,8,256]{3,2,1,0:T(8,128)S(1)} %get-tuple-element.23), channel_id=1, source_target_pairs={{0,4},{4,8},{8,12},{12,16},{16,20},{20,24},{24,28},{28,32},{32,36}... | collective-permute-start | bytes 393224 | tf_op jit(solution)/shard_map/ppermute | solution.py:19
  18.8 14.8 %collective-permute-start.2 = (f32[16,1,8,256]{3,2,1,0:T(8,128)S(1)}, f32[16,1,8,256]{3,2,1,0:T(8,128)S(1)}, u32[]{:S(2)}, u32[]{:S(2)}) collective-permute-start(f32[16,1,8,256]{3,2,1,0:T(8,128)S(1)} %get-tuple-element.22), channel_id=1, source_target_pairs={{4,0},{8,4},{12,8},{16,12},{20,16},{24,20},{28,24},{32,28},{36,32}... | collective-permute-start | bytes 393224 | tf_op jit(solution)/shard_map/ppermute | solution.py:22
  32.4 1.1 copy-start.7
  32.4 2.0 copy-start
  33.5 28.2 %copy-start.1 = (f32[24,8,256]{2,1,0:T(8,128)}, f32[24,8,256]{2,1,0:T(8,128)S(1)}, u32[]{:S(2)}) copy-start(f32[24,8,256]{2,1,0:T(8,128)S(1)} %get-tuple-element.28) | copy-start | bytes 589828
  33.5 28.2 %copy-start.3 = (f32[24,8,256]{2,1,0:T(8,128)}, f32[24,8,256]{2,1,0:T(8,128)S(1)}, u32[]{:S(2)}) copy-start(f32[24,8,256]{2,1,0:T(8,128)S(1)} %get-tuple-element.29) | copy-start | bytes 589828
  33.6 28.2 %copy-start.5 = (f32[24,8,256]{2,1,0:T(8,128)}, f32[24,8,256]{2,1,0:T(8,128)S(1)}, u32[]{:S(2)}) copy-start(f32[24,8,256]{2,1,0:T(8,128)S(1)} %get-tuple-element.32) | copy-start | bytes 589828
  35.8 11.3 %collective-permute-start.3 = (f32[16,1,8,256]{3,2,1,0:T(8,128)S(1)}, f32[16,1,8,256]{3,2,1,0:T(8,128)S(1)}, u32[]{:S(2)}, u32[]{:S(2)}) collective-permute-start(f32[16,1,8,256]{3,2,1,0:T(8,128)S(1)} %get-tuple-element.21), channel_id=1, source_target_pairs={{0,4},{4,8},{8,12},{12,16},{16,20},{20,24},{24,28},{28,32},{32,36}... | collective-permute-start | bytes 393224 | tf_op jit(solution)/shard_map/ppermute | solution.py:19
  35.9 11.2 %collective-permute-start.4 = (f32[16,1,8,256]{3,2,1,0:T(8,128)S(1)}, f32[16,1,8,256]{3,2,1,0:T(8,128)S(1)}, u32[]{:S(2)}, u32[]{:S(2)}) collective-permute-start(f32[16,1,8,256]{3,2,1,0:T(8,128)S(1)} %get-tuple-element.20), channel_id=1, source_target_pairs={{4,0},{8,4},{12,8},{16,12},{20,16},{24,20},{28,24},{32,28},{36,32}... | collective-permute-start | bytes 393224 | tf_op jit(solution)/shard_map/ppermute | solution.py:22
  47.2 0.9 copy-start.8
  51.0 10.8 %collective-permute-start.5 = (f32[16,1,8,256]{3,2,1,0:T(8,128)S(1)}, f32[16,1,8,256]{3,2,1,0:T(8,128)S(1)}, u32[]{:S(2)}, u32[]{:S(2)}) collective-permute-start(f32[16,1,8,256]{3,2,1,0:T(8,128)S(1)} %get-tuple-element.18), channel_id=1, source_target_pairs={{0,4},{4,8},{8,12},{12,16},{16,20},{20,24},{24,28},{28,32},{32,36}... | collective-permute-start | bytes 393224 | tf_op jit(solution)/shard_map/ppermute | solution.py:19
  51.0 10.7 %collective-permute-start.6 = (f32[16,1,8,256]{3,2,1,0:T(8,128)S(1)}, f32[16,1,8,256]{3,2,1,0:T(8,128)S(1)}, u32[]{:S(2)}, u32[]{:S(2)}) collective-permute-start(f32[16,1,8,256]{3,2,1,0:T(8,128)S(1)} %get-tuple-element.19), channel_id=1, source_target_pairs={{4,0},{8,4},{12,8},{16,12},{20,16},{24,20},{28,24},{32,28},{36,32}... | collective-permute-start | bytes 393224 | tf_op jit(solution)/shard_map/ppermute | solution.py:22
  64.0 10.8 %collective-permute-start.7 = (f32[16,1,8,256]{3,2,1,0:T(8,128)S(1)}, f32[16,1,8,256]{3,2,1,0:T(8,128)S(1)}, u32[]{:S(2)}, u32[]{:S(2)}) collective-permute-start(f32[16,1,8,256]{3,2,1,0:T(8,128)S(1)} %get-tuple-element.14), channel_id=1, source_target_pairs={{0,4},{4,8},{8,12},{12,16},{16,20},{20,24},{24,28},{28,32},{32,36}... | collective-permute-start | bytes 393224 | tf_op jit(solution)/shard_map/ppermute | solution.py:19
  64.1 10.7 %copy-start.2 = (f32[24,8,256]{2,1,0:T(8,128)S(1)}, f32[24,8,256]{2,1,0:T(8,128)}, u32[]{:S(2)}) copy-start(f32[24,8,256]{2,1,0:T(8,128)} %copy-done.1) | copy-start | bytes 589828
  64.1 10.7 %copy-start.4 = (f32[24,8,256]{2,1,0:T(8,128)S(1)}, f32[24,8,256]{2,1,0:T(8,128)}, u32[]{:S(2)}) copy-start(f32[24,8,256]{2,1,0:T(8,128)} %copy-done.3) | copy-start | bytes 589828
  64.1 10.7 %copy-start.6 = (f32[24,8,256]{2,1,0:T(8,128)S(1)}, f32[24,8,256]{2,1,0:T(8,128)}, u32[]{:S(2)}) copy-start(f32[24,8,256]{2,1,0:T(8,128)} %copy-done.5) | copy-start | bytes 589828
  64.1 10.6 %collective-permute-start.8 = (f32[16,1,8,256]{3,2,1,0:T(8,128)S(1)}, f32[16,1,8,256]{3,2,1,0:T(8,128)S(1)}, u32[]{:S(2)}, u32[]{:S(2)}) collective-permute-start(f32[16,1,8,256]{3,2,1,0:T(8,128)S(1)} %get-tuple-element.15), channel_id=1, source_target_pairs={{4,0},{8,4},{12,8},{16,12},{20,16},{24,20},{28,24},{32,28},{36,32}... | collective-permute-start | bytes 393224 | tf_op jit(solution)/shard_map/ppermute | solution.py:22
Sparse Core Ops, SparseCore 0:
  110.4 116.1 all-gather.2
